TPU v7x, 32 devices: a whole 2x2x4 slice. The times are simulated.
32 devices in a mesh: obs: 4 (over z), src: 8 (over y, x, core).
Axes of the slice: x: 2, y: 2, z: 4, core: 2. Of those that a mesh axis runs over, the one named last changes fastest.
Arguments:
- history: bfloat16 [3, 64, 64, 1536], P(None, ('obs', 'src')), may hold values from -6 to 6
- incident: bfloat16 [5, 64, 64, 1536], P(None, ('obs', 'src')), may hold values from -6 to 6
- proj_basis: bfloat16 [64, 64, 1536], P(('obs', 'src')), may hold values from -0.15625 to 0.15625
- expand_basis: bfloat16 [64, 64, 1536], P(('obs', 'src')), may hold values from -0.75 to 0.75
- near_inverse: bfloat16 [64, 1536, 1536], P(('obs', 'src')), may hold values from -0.15625 to 0.15625
- couplings: bfloat16 [2, 4096, 4, 8, 128], P(None, 'obs', None, 'src'), may hold values from -0.09375 to 0.09375
- lags: int32 [64, 4, 8, 2], P('obs', None, 'src'), may hold values from 0 to 2, as said below
Outputs:
- currents: bfloat16 [5, 64, 64, 1536], P(None, ('obs', 'src'))
Inputs may be any that keep to these rules, and one draw needn't show every extreme that they name: lags[j, o, s, k] is the lag from source cluster j to observer cluster (o * 8 + s) * 2 + k. Entries are 0, 1 or 2, and the entry of every cluster with itself is 0.
All inputs are finite; a program needn't handle non-finite values.
Results may differ from a plain program's by a relative error of at most 0.025.
Values may be sent and summed in bfloat16 or wider, within the bound.
A program may use at most 192 MiB of HBM per device.

v0:
```python
import jax
import jax.numpy as jnp
from jax import lax
from jax.sharding import PartitionSpec as P

STEPS = 5
TAPS = 2
HIST = 3


def per_device(history, incident, proj_basis, expand_basis, near_inverse, couplings, lags):
    rank = proj_basis.shape[1]
    local_clusters = proj_basis.shape[0]
    excite = history.shape[2]
    src_rows = couplings.shape[1]
    obs_cols = couplings.shape[2] * couplings.shape[3] * couplings.shape[4]
    src_clusters = lags.shape[0]
    obs_clusters = lags.shape[1] * lags.shape[2] * lags.shape[3]
    kernel = couplings.reshape(TAPS, src_clusters, rank, obs_clusters, rank)
    lag_pairs = lags.reshape(src_clusters, obs_clusters)
    matrices = []
    for delay in range(1, HIST + 1):
        combined = jnp.zeros_like(kernel[0])
        for tap_index in range(TAPS):
            if delay - tap_index >= 1:
                chosen = (lag_pairs == delay - tap_index)[:, None, :, None]
                combined = jnp.where(chosen, kernel[tap_index], combined)
        matrices.append(combined.reshape(src_rows, obs_cols))

    def project(current):
        projected = jnp.einsum(
            "ceb,crb->ecr", current, proj_basis, preferred_element_type=jnp.float32
        )
        return projected.astype(jnp.bfloat16).reshape(excite, local_clusters * rank)

    def couple(columns, delay):
        return jnp.dot(columns, matrices[delay - 1], preferred_element_type=jnp.float32)

    stacked = jnp.stack([project(history[slot_index]) for slot_index in range(HIST)])
    gathered = lax.all_gather(stacked, "src", axis=2, tiled=True)
    past = [gathered[slot_index] for slot_index in range(HIST)]
    results = []
    latest = None
    for step in range(STEPS):
        if step > 0:
            newest = lax.all_gather(latest, "src", axis=1, tiled=True)
            past = past[1:] + [newest]
        partial_value = couple(past[-1], 1) + couple(past[-2], 2) + couple(past[-3], 3)
        field = lax.psum_scatter(
            partial_value.astype(jnp.bfloat16), "obs", scatter_dimension=1, tiled=True
        )
        field_cast = field.reshape(excite, local_clusters, rank)
        far_field = jnp.einsum(
            "ecr,crb->ceb", field_cast, expand_basis, preferred_element_type=jnp.float32
        )
        residual_field = (incident[step].astype(jnp.float32) - far_field).astype(jnp.bfloat16)
        current = jnp.einsum(
            "ceb,cbd->ced", residual_field, near_inverse, preferred_element_type=jnp.float32
        ).astype(jnp.bfloat16)
        results.append(current)
        if step + 1 < STEPS:
            latest = project(current)
    return jnp.stack(results)


def solution(mesh):
    placed = (
        P(None, ("obs", "src"), None, None),
        P(None, ("obs", "src"), None, None),
        P(("obs", "src"), None, None),
        P(("obs", "src"), None, None),
        P(("obs", "src"), None, None),
        P(None, "obs", None, "src", None),
        P("obs", None, "src", None),
    )
    return jax.shard_map(
        per_device,
        mesh=mesh,
        in_specs=placed,
        out_specs=P(None, ("obs", "src"), None, None),
        check_vma=False,
    )
```

profile of v0, /device:TPU:0, one launch (start us, length us, event | category | flops | bytes accessed | tf_op | source)
XLA Modules:
  0.0 237.1 jit_solution(1757093044412803134)
XLA Ops:
  11.1 2.3 fusion.46
  13.3 2.0 squeeze.40
  15.3 1.8 squeeze.42
  17.2 4.3 %select_select_fusion = (bf16[16,64,8,64]{3,2,1,0:T(8,128)(2,1)}, bf16[16,64,8,64]{3,2,1,0:T(8,128)(2,1)}, bf16[16,64,8,64]{3,2,1,0:T(8,128)(2,1)}) fusion(bf16[16,64,8,64]{3,2,1,0:T(8,128)(2,1)} %squeeze.42, bf16[16,64,8,64]{3,2,1,0:T(8,128)(2,1)} %squeeze.40, pred[16,8]{1,0:T(8,128)(4,1)S(1)} %copy.20, pred[16,8]{1,0:T(8,128)(4,1)S(1)} %copy.19, ...), kind=kLoop, calls=%fused_computation.17 | loop fusion | flops 2621440 | bytes 5243264 | tf_op jit(solution)/shard_map/jit(_where)/select_n | solution.py:27
  21.5 4.0 %select_n.97 = bf16[1024,512]{1,0:T(8,128)(2,1)} reshape(bf16[16,64,8,64]{3,2,1,0:T(8,128)(2,1)} %get-tuple-element.7) | data formatting | bytes 2097152 | tf_op jit(solution)/shard_map/jit(_where)/select_n | solution.py:27
  25.6 11.9 %all_gather.15 = bf16[3,64,1024]{1,2,0:T(8,128)(2,1)S(1)} all-gather(bf16[3,64,128]{1,2,0:T(8,128)(2,1)S(1)} %pad_maximum_fusion), channel_id=1, replica_groups=mesh['obs'=4,'src'=8] {'src'}, dimensions={2}, use_global_device_ids=true | all-gather | bytes 442368 | tf_op jit(solution)/shard_map/all_gather | solution.py:40
  37.5 3.5 %select_n.100 = bf16[1024,512]{1,0:T(8,128)(2,1)S(1)} reshape(bf16[16,64,8,64]{3,2,1,0:T(8,128)(2,1)} %get-tuple-element.6) | data formatting | bytes 2097152 | tf_op jit(solution)/shard_map/jit(_where)/select_n | solution.py:27
  41.0 3.2 %select_n.103 = bf16[1024,512]{1,0:T(8,128)(2,1)S(1)} reshape(bf16[16,64,8,64]{3,2,1,0:T(8,128)(2,1)} %get-tuple-element.5) | data formatting | bytes 2097152 | tf_op jit(solution)/shard_map/jit(_where)/select_n | solution.py:27
  48.5 2.7 %broadcast_in_dim.38 = pred[1024,512]{1,0:T(32,128)(4,1)} reshape(pred[16,64,8,64]{3,2,1,0:T(8,128)(4,1)S(1)} %broadcast_in_dim.35) | data formatting | bytes 1048576 | tf_op jit(solution)/shard_map/jit(_where)/broadcast_in_dim | solution.py:27
  51.6 2.7 %broadcast_in_dim.39 = pred[1024,512]{1,0:T(32,128)(4,1)} reshape(pred[16,64,8,64]{3,2,1,0:T(8,128)(4,1)S(1)} %broadcast_in_dim.36) | data formatting | bytes 1048576 | tf_op jit(solution)/shard_map/jit(_where)/broadcast_in_dim | solution.py:27
  54.3 2.5 %bitcast_select_fusion.1 = bf16[1024,512]{1,0:T(8,128)(2,1)S(1)} fusion(pred[1024,512]{1,0:T(32,128)(4,1)} %broadcast_in_dim.38, pred[1024,512]{1,0:T(32,128)(4,1)} %broadcast_in_dim.39, bf16[128,8,4,128]{3,2,1,0:T(4,128)(2,1)} %bitcast.199, bf16[128,8,4,128]{3,2,1,0:T(4,128)(2,1)} %bitcast.202), kind=kLoop, calls=%fused_computation.47 | loop fusion | flops 1048576 | bytes 4194304 | tf_op jit(solution)/shard_map/jit(_where)/select_n | solution.py:27
  56.8 1.9 fusion.41
  58.8 8.2 %reduce-scatter.16.cloned.1.call-done = bf16[128,64]{1,0:T(8,128)(2,1)} async-done(((bf16[512,64]{1,0:T(8,128)(2,1)}), bf16[128,64]{1,0:T(8,128)(2,1)}) %reduce-scatter.16.cloned.1.call-update) | async-done | bytes 16400
  67.0 6.7 %bitcast_dynamic-update-slice_fusion.3 = (bf16[5,2,64,1536]{3,2,1,0:T(8,128)(2,1)}, bf16[2,64,1536]{2,1,0:T(8,128)(2,1)}) fusion(bf16[2,1536,1536]{2,1,0:T(8,128)(2,1)} %param.11, bf16[64,2,64]{0,2,1:T(8,128)(2,1)} %bitcast.214, bf16[2,64,1536]{2,1,0:T(8,128)(2,1)S(1)} %copy-done, bf16[5,2,64,1536]{3,2,1,0:T(8,128)(2,1)} %param.8), kind=kOutput, calls=%fused_computation.64 | convolution fusion | flops 629932032 | bytes 11042816 | tf_op jit(solution)/shard_map/ceb,cbd->ced/dot_general | solution.py:57
  76.6 9.2 %all_gather.16 = bf16[64,1024]{1,0:T(8,128)(2,1)S(1)} all-gather(bf16[64,128]{1,0:T(8,128)(2,1)S(1)} %reshape.176), channel_id=1, replica_groups=mesh['obs'=4,'src'=8] {'src'}, dimensions={1}, use_global_device_ids=true | all-gather | bytes 147456 | tf_op jit(solution)/shard_map/all_gather | solution.py:46
  86.5 2.3 fusion.13
  88.7 1.6 copy.32
  90.4 1.9 fusion.40
  92.3 14.9 %reduce-scatter.18.cloned.1.call-done = bf16[128,64]{1,0:T(8,128)(2,1)} async-done(((bf16[512,64]{1,0:T(8,128)(2,1)}), bf16[128,64]{1,0:T(8,128)(2,1)}) %reduce-scatter.18.cloned.1.call-update) | async-done | bytes 16400
  107.2 6.7 %bitcast_dynamic-update-slice_fusion.2 = (bf16[5,2,64,1536]{3,2,1,0:T(8,128)(2,1)}, bf16[2,64,1536]{2,1,0:T(8,128)(2,1)}) fusion(bf16[5,2,64,1536]{3,2,1,0:T(8,128)(2,1)} %get-tuple-element.13, bf16[2,1536,1536]{2,1,0:T(8,128)(2,1)} %param.11, bf16[64,2,64]{0,2,1:T(8,128)(2,1)} %bitcast.216, bf16[2,64,1536]{2,1,0:T(8,128)(2,1)S(1)} %copy-done, ...), kind=kOutput, calls=%fused_computation.63 | convolution fusion | flops 629932032 | bytes 11042816 | tf_op jit(solution)/shard_map/ceb,cbd->ced/dot_general | solution.py:57
  116.7 9.1 %all_gather.17 = bf16[64,1024]{1,0:T(8,128)(2,1)S(1)} all-gather(bf16[64,128]{1,0:T(8,128)(2,1)S(1)} %reshape.178), channel_id=1, replica_groups=mesh['obs'=4,'src'=8] {'src'}, dimensions={1}, use_global_device_ids=true | all-gather | bytes 147456 | tf_op jit(solution)/shard_map/all_gather | solution.py:46
  129.0 4.0 %broadcast_in_dim.40 = pred[1024,512]{1,0:T(32,128)(4,1)} reshape(pred[16,64,8,64]{3,2,1,0:T(8,128)(4,1)} %broadcast_in_dim.37) | data formatting | bytes 1048576 | tf_op jit(solution)/shard_map/jit(_where)/broadcast_in_dim | solution.py:27
  133.0 11.5 %reduce-scatter.20.cloned.1.call-done = bf16[128,64]{1,0:T(8,128)(2,1)} async-done(((bf16[512,64]{1,0:T(8,128)(2,1)}), bf16[128,64]{1,0:T(8,128)(2,1)}) %reduce-scatter.20.cloned.1.call-update) | async-done | bytes 16400
  144.5 6.6 %bitcast_dynamic-update-slice_fusion.1 = (bf16[5,2,64,1536]{3,2,1,0:T(8,128)(2,1)}, bf16[2,64,1536]{2,1,0:T(8,128)(2,1)S(1)}) fusion(bf16[5,2,64,1536]{3,2,1,0:T(8,128)(2,1)} %get-tuple-element.15, bf16[2,1536,1536]{2,1,0:T(8,128)(2,1)} %param.11, bf16[64,2,64]{0,2,1:T(8,128)(2,1)} %bitcast.215, bf16[2,64,1536]{2,1,0:T(8,128)(2,1)S(1)} %copy-done, ...), kind=kOutput, calls=%fused_computation.62 | convolution fusion | flops 629932032 | bytes 11042816 | tf_op jit(solution)/shard_map/ceb,cbd->ced/dot_general | solution.py:57
  152.9 9.1 %all_gather.18 = bf16[64,1024]{1,0:T(8,128)(2,1)S(1)} all-gather(bf16[64,128]{1,0:T(8,128)(2,1)S(1)} %reshape.180), channel_id=1, replica_groups=mesh['obs'=4,'src'=8] {'src'}, dimensions={1}, use_global_device_ids=true | all-gather | bytes 147456 | tf_op jit(solution)/shard_map/all_gather | solution.py:46
  162.7 1.6 fusion.44
  166.1 1.6 copy.36
  167.8 16.8 %reduce-scatter.22.cloned.1.call-done = bf16[128,64]{1,0:T(8,128)(2,1)} async-done(((bf16[512,64]{1,0:T(8,128)(2,1)}), bf16[128,64]{1,0:T(8,128)(2,1)}) %reduce-scatter.22.cloned.1.call-update) | async-done | bytes 16400
  184.6 6.7 %bitcast_dynamic-update-slice_fusion = (bf16[5,2,64,1536]{3,2,1,0:T(8,128)(2,1)}, bf16[2,64,1536]{2,1,0:T(8,128)(2,1)}) fusion(bf16[5,2,64,1536]{3,2,1,0:T(8,128)(2,1)} %get-tuple-element.17, bf16[2,1536,1536]{2,1,0:T(8,128)(2,1)} %param.11, bf16[64,2,64]{0,2,1:T(8,128)(2,1)} %bitcast.217, bf16[2,64,1536]{2,1,0:T(8,128)(2,1)S(1)} %copy-done, ...), kind=kOutput, calls=%fused_computation.61 | convolution fusion | flops 629932032 | bytes 11042816 | tf_op jit(solution)/shard_map/ceb,cbd->ced/dot_general | solution.py:57
  194.2 9.4 %all_gather.19 = bf16[64,1024]{1,0:T(8,128)(2,1)S(1)} all-gather(bf16[64,128]{1,0:T(8,128)(2,1)S(1)} %reshape.182), channel_id=1, replica_groups=mesh['obs'=4,'src'=8] {'src'}, dimensions={1}, use_global_device_ids=true | all-gather | bytes 147456 | tf_op jit(solution)/shard_map/all_gather | solution.py:46
  207.1 16.9 %reduce-scatter.24.cloned.1.call-done = bf16[128,64]{1,0:T(8,128)(2,1)} async-done(((bf16[512,64]{1,0:T(8,128)(2,1)}), bf16[128,64]{1,0:T(8,128)(2,1)}) %reduce-scatter.24.cloned.1.call-update) | async-done | bytes 16400
  224.0 6.6 %fusion.6 = bf16[5,2,64,1536]{3,2,1,0:T(8,128)(2,1)} fusion(bf16[5,2,64,1536]{3,2,1,0:T(8,128)(2,1)} %get-tuple-element.19, bf16[2,1536,1536]{2,1,0:T(8,128)(2,1)} %param.11, bf16[64,2,64]{0,2,1:T(8,128)(2,1)} %bitcast.218, bf16[2,64,1536]{2,1,0:T(8,128)(2,1)S(1)} %copy-done, bf16[5,2,64,1536]{3,2,1,0:T(8,128)(2,1)} %param.8), kind=kOutput, calls=%fused_computation.16 | convolution fusion | flops 629932032 | bytes 10649600 | tf_op jit(solution)/shard_map/ceb,cbd->ced/dot_general | solution.py:57
  (98 shorter events, 29.2 us)
Async XLA Ops:
  6.5 60.5 %copy-start = (bf16[2,64,1536]{2,1,0:T(8,128)(2,1)S(1)}, bf16[2,64,1536]{2,1,0:T(8,128)(2,1)}, u32[]{:S(2)}) copy-start(bf16[2,64,1536]{2,1,0:T(8,128)(2,1)} %param.10) | copy-start | bytes 1179652
  6.5 4.2 %copy-start.23 = (s32[16,4,1,2]{0,3,2,1:T(2,128)S(1)}, s32[16,4,1,2]{0,3,2,1:T(2,128)}, u32[]{:S(2)}) copy-start(s32[16,4,1,2]{0,3,2,1:T(2,128)} %param.13) | copy-start | bytes 1540
  6.5 60.5 %reduce-scatter.16.cloned.1.call-start = ((), (), s32[]{:S(2)}) async-start(), calls=%async_computation.5 | async-start | bytes 163840
  11.1 6.1 %copy-start.21 = (pred[16,8]{1,0:T(8,128)(4,1)}, pred[16,8]{1,0:T(8,128)(4,1)S(1)}, u32[]{:S(2)}) copy-start(pred[16,8]{1,0:T(8,128)(4,1)S(1)} %copy.20) | copy-start | bytes 388
  13.3 3.8 %copy-start.1 = (bf16[1,1024,4,1,128]{4,2,3,1,0:T(4,128)(2,1)}, bf16[1,1024,4,1,128]{4,2,3,1,0:T(4,128)(2,1)S(1)}, u32[]{:S(2)}) copy-start(bf16[1,1024,4,1,128]{4,2,3,1,0:T(4,128)(2,1)S(1)} %get-tuple-element.8) | copy-start | bytes 3145732
  13.3 3.8 %copy-start.3 = (bf16[1,1024,4,1,128]{4,2,3,1,0:T(4,128)(2,1)}, bf16[1,1024,4,1,128]{4,2,3,1,0:T(4,128)(2,1)S(1)}, u32[]{:S(2)}) copy-start(bf16[1,1024,4,1,128]{4,2,3,1,0:T(4,128)(2,1)S(1)} %get-tuple-element.9) | copy-start | bytes 3145732
  37.5 9.7 %copy-start.5 = (bf16[3,64,1024]{1,2,0:T(8,128)(2,1)}, bf16[3,64,1024]{1,2,0:T(8,128)(2,1)S(1)}, u32[]{:S(2)}) copy-start(bf16[3,64,1024]{1,2,0:T(8,128)(2,1)S(1)} %all_gather.15) | copy-start | bytes 1179652
  47.1 60.1 %reduce-scatter.18.cloned.1.call-start = ((), (), s32[]{:S(2)}) async-start(), calls=%async_computation.6 | async-start | bytes 163840
  67.0 19.4 %copy-start.4 = (bf16[1,1024,4,1,128]{4,2,3,1,0:T(4,128)(2,1)S(1)}, bf16[1,1024,4,1,128]{4,2,3,1,0:T(4,128)(2,1)}, u32[]{:S(2)}) copy-start(bf16[1,1024,4,1,128]{4,2,3,1,0:T(4,128)(2,1)} %copy-done.3) | copy-start | bytes 3145732
  85.8 0.6 copy-start.12
  90.4 54.2 %reduce-scatter.20.cloned.1.call-start = ((), (), s32[]{:S(2)}) async-start(), calls=%async_computation.7 | async-start | bytes 163840
  107.2 6.8 %copy-start.6 = (bf16[2,64,1536]{2,1,0:T(8,128)(2,1)S(1)}, bf16[2,64,1536]{2,1,0:T(8,128)(2,1)}, u32[]{:S(2)}) copy-start(bf16[2,64,1536]{2,1,0:T(8,128)(2,1)} %param.9) | copy-start | bytes 1179652
  107.2 18.7 %copy-start.9 = (pred[1024,512]{1,0:T(32,128)(4,1)S(1)}, pred[1024,512]{1,0:T(32,128)(4,1)}, u32[]{:S(2)}) copy-start(pred[1024,512]{1,0:T(32,128)(4,1)} %broadcast_in_dim.38) | copy-start | bytes 1572868
  114.0 12.6 %copy-start.13 = (bf16[64,1024]{1,0:T(8,128)(2,1)S(1)}, bf16[64,1024]{1,0:T(8,128)(2,1)}, u32[]{:S(2)}) copy-start(bf16[64,1024]{1,0:T(8,128)(2,1)} %copy-done.12) | copy-start | bytes 393220
  116.7 9.8 %copy-start.15 = (f32[64,512]{1,0:T(8,128)S(1)}, f32[64,512]{1,0:T(8,128)}, u32[]{:S(2)}) copy-start(f32[64,512]{1,0:T(8,128)} %fusion.40) | copy-start | bytes 393220
  125.9 0.7 copy-start.16
  125.9 1.8 copy-start.22
  127.6 57.0 %reduce-scatter.22.cloned.1.call-start = ((), (), s32[]{:S(2)}) async-start(), calls=%async_computation.8 | async-start | bytes 163840
  152.0 12.7 %copy-start.2 = (bf16[1,1024,4,1,128]{4,2,3,1,0:T(4,128)(2,1)S(1)}, bf16[1,1024,4,1,128]{4,2,3,1,0:T(4,128)(2,1)}, u32[]{:S(2)}) copy-start(bf16[1,1024,4,1,128]{4,2,3,1,0:T(4,128)(2,1)} %copy-done.1) | copy-start | bytes 3145732
  152.9 11.4 %copy-start.17 = (bf16[64,1024]{1,0:T(8,128)(2,1)S(1)}, bf16[64,1024]{1,0:T(8,128)(2,1)}, u32[]{:S(2)}) copy-start(bf16[64,1024]{1,0:T(8,128)(2,1)} %copy-done.16) | copy-start | bytes 393220
  152.9 11.7 %copy-start.7 = (pred[1024,512]{1,0:T(32,128)(4,1)S(1)}, pred[1024,512]{1,0:T(32,128)(4,1)}, u32[]{:S(2)}) copy-start(pred[1024,512]{1,0:T(32,128)(4,1)} %broadcast_in_dim.39) | copy-start | bytes 1572868
  152.9 11.7 %copy-start.10 = (pred[1024,512]{1,0:T(32,128)(4,1)S(1)}, pred[1024,512]{1,0:T(32,128)(4,1)}, u32[]{:S(2)}) copy-start(pred[1024,512]{1,0:T(32,128)(4,1)} %broadcast_in_dim.40) | copy-start | bytes 1572868
  152.9 11.7 %copy-start.14 = (bf16[64,1024]{1,0:T(8,128)(2,1)S(1)}, bf16[64,1024]{1,0:T(8,128)(2,1)}, u32[]{:S(2)}) copy-start(bf16[64,1024]{1,0:T(8,128)(2,1)} %copy-done.12) | copy-start | bytes 393220
  162.1 0.7 copy-start.19
  167.8 56.2 %reduce-scatter.24.cloned.1.call-start = ((), (), s32[]{:S(2)}) async-start(), calls=%async_computation.9 | async-start | bytes 163840
  194.1 11.0 %copy-start.20 = (bf16[64,1024]{1,0:T(8,128)(2,1)S(1)}, bf16[64,1024]{1,0:T(8,128)(2,1)}, u32[]{:S(2)}) copy-start(bf16[64,1024]{1,0:T(8,128)(2,1)} %copy-done.19) | copy-start | bytes 393220
  194.1 11.3 %copy-start.8 = (pred[1024,512]{1,0:T(32,128)(4,1)S(1)}, pred[1024,512]{1,0:T(32,128)(4,1)}, u32[]{:S(2)}) copy-start(pred[1024,512]{1,0:T(32,128)(4,1)} %broadcast_in_dim.39) | copy-start | bytes 1572868
  194.2 11.3 %copy-start.11 = (pred[1024,512]{1,0:T(32,128)(4,1)S(1)}, pred[1024,512]{1,0:T(32,128)(4,1)}, u32[]{:S(2)}) copy-start(pred[1024,512]{1,0:T(32,128)(4,1)} %broadcast_in_dim.40) | copy-start | bytes 1572868
  194.2 11.3 %copy-start.18 = (bf16[64,1024]{1,0:T(8,128)(2,1)S(1)}, bf16[64,1024]{1,0:T(8,128)(2,1)}, u32[]{:S(2)}) copy-start(bf16[64,1024]{1,0:T(8,128)(2,1)} %copy-done.16) | copy-start | bytes 393220
Sparse Core Ops, SparseCore 0:
  47.3 19.7 reduce-scatter.15
  90.5 16.6 reduce-scatter.17
  127.7 16.7 reduce-scatter.19
  167.9 16.6 reduce-scatter.21
  207.3 16.6 reduce-scatter.23
where the time goes:
time: 238 us; the launch traced here: 237 us
  waiting for transfers between devices  68.4 us (29%)
  matrix products  57.8 us (24%)
  blocking collectives  48.8 us (21%)
  local copies, waits for them, and re-layouts  41.5 us (17%)
  between operations  13.5 us (6%)
  other arithmetic  6.91 us (3%)
    unnamed x10, waiting for transfers between devices  68.4 us
    all_gather x4, blocking collectives, per_device(): newest = lax.all_gather(latest, 'src', axis=1, tiled=True)  36.9 us
    dot_general x5, matrix products, per_device(): jnp.einsum('ceb,cbd->ced', residual_field, near_inverse, preferred_elemen...  33.3 us
    dot_general x15, matrix products, couple(): jnp.dot(columns, matrices[delay - 1], preferred_element_type=jnp.float32)  16.1 us
    all_gather x1, blocking collectives, per_device(): gathered = lax.all_gather(stacked, 'src', axis=2, tiled=True)  11.9 us
    broadcast_in_dim x6, local copies, waits for them, and re-layouts, per_device(): combined = jnp.where(chosen, kernel[tap_index], combined)  11.4 us
    select_n x3, local copies, waits for them, and re-layouts, per_device(): combined = jnp.where(chosen, kernel[tap_index], combined)  10.7 us
    dot_general x7, matrix products, project(): jnp.einsum('ceb,crb->ecr', current, proj_basis, preferred_element_type=jn...  8.37 us
  transfers between devices with their start and end apart: 5, of which 5 were waited for; matrix products, arithmetic and copies ran while one was open for 8% of the time, Pallas kernels for 0%

commit v1 on v0

--- a/solution.py
+++ b/solution.py
@@ -6,6 +6,27 @@
 STEPS = 5
 TAPS = 2
 HIST = 3
+
+
+def ring_gather(shard, axis, dim):
+    peers, place, rows = (lax.axis_size(axis), lax.axis_index(axis), shard.shape[dim])
+    right = [(i, (i + 1) % peers) for i in range(peers)]
+    downward = [(i, (i - 1) % peers) for i in range(peers)]
+    out = jnp.zeros((*shard.shape[:dim], peers * rows, *shard.shape[dim + 1 :]), shard.dtype)
+    out = lax.dynamic_update_slice_in_dim(out, shard, place * rows, axis=dim)
+    from_left = from_right = shard
+    half = peers // 2
+    for step in range(1, half + 1):
+        from_left = lax.ppermute(from_left, axis, right)
+        out = lax.dynamic_update_slice_in_dim(
+            out, from_left, (place - step) % peers * rows, axis=dim
+        )
+        if step < peers - half:
+            from_right = lax.ppermute(from_right, axis, downward)
+            out = lax.dynamic_update_slice_in_dim(
+                out, from_right, (place + step) % peers * rows, axis=dim
+            )
+    return out
 
 
 def per_device(history, incident, proj_basis, expand_basis, near_inverse, couplings, lags):
@@ -43,7 +64,7 @@
     latest = None
     for step in range(STEPS):
         if step > 0:
-            newest = lax.all_gather(latest, "src", axis=1, tiled=True)
+            newest = ring_gather(latest, "src", 1)
             past = past[1:] + [newest]
         partial_value = couple(past[-1], 1) + couple(past[-2], 2) + couple(past[-3], 3)
         field = lax.psum_scatter(

time: 238 us -> 259 us (1.088)
  blocking collectives: 48.8 us -> 11.9 us
  starting transfers between devices: 0.17 us -> 32.5 us
  waiting for transfers between devices: 68.4 us -> 99.3 us
  local copies, waits for them, and re-layouts: 41.5 us -> 32.1 us
  matrix products: 57.8 us -> 62.4 us
    all_gather x4 -> x0, blocking collectives: 36.9 us -> none  [per_device(): newest = lax.all_gather(latest, 'src', axis=1, tiled=True)]
    ppermute x0 -> x28, waiting for transfers between devices: none -> 32.9 us  [the longest x16 32.3 us: ring_gather(): from_left = lax.ppermute(from_left, axis, right)]
    ppermute x0 -> x28, starting transfers between devices: none -> 31.9 us  [the longest x12 31.7 us: ring_gather(): from_right = lax.ppermute(from_right, axis, downward)]
    dot_general x15, matrix products: 16.1 us -> 20.6 us  [couple(): jnp.dot(columns, matrices[delay - 1], preferred_element_type=jnp.float32)]
    broadcast_in_dim x6, local copies, waits for them, and re-layouts: 11.4 us -> 7.93 us  [per_device(): combined = jnp.where(chosen, kernel[tap_index], combined)]
    unnamed x53 -> x31, local copies, waits for them, and re-layouts: 6.97 us -> 6.99 us
  transfers between devices with their start and end apart: 5 -> 33, of which waited for: 5 -> 27; matrix products, arithmetic and copies ran while one was open for 8% -> 8% of each run, Pallas kernels for 0% -> 0%
where the time goes in v1:
time: 259 us; the launch traced here: 258 us
  waiting for transfers between devices  99.3 us (38%)
  matrix products  62.4 us (24%)
  starting transfers between devices  32.5 us (13%)
  local copies, waits for them, and re-layouts  32.1 us (12%)
  between operations  13.5 us (5%)
  blocking collectives  11.9 us (5%)
  other arithmetic  6.51 us (3%)
    unnamed x10, waiting for transfers between devices  66.4 us
    dot_general x5, matrix products, per_device(): jnp.einsum('ceb,cbd->ced', residual_field, near_inverse, preferred_elemen...  33.3 us
    ppermute x16, waiting for transfers between devices, ring_gather(): from_left = lax.ppermute(from_left, axis, right)  32.3 us
    ppermute x12, starting transfers between devices, ring_gather(): from_right = lax.ppermute(from_right, axis, downward)  31.7 us
    dot_general x15, matrix products, couple(): jnp.dot(columns, matrices[delay - 1], preferred_element_type=jnp.float32)  20.6 us
    all_gather x1, blocking collectives, per_device(): gathered = lax.all_gather(stacked, 'src', axis=2, tiled=True)  11.9 us
    select_n x3, local copies, waits for them, and re-layouts, per_device(): combined = jnp.where(chosen, kernel[tap_index], combined)  8.7 us
    dot_general x7, matrix products, project(): jnp.einsum('ceb,crb->ecr', current, proj_basis, preferred_element_type=jn...  8.42 us
  transfers between devices with their start and end apart: 33, of which 27 were waited for; matrix products, arithmetic and copies ran while one was open for 8% of the time, Pallas kernels for 0%

profile of v1, /device:TPU:0, one launch (start us, length us, event | category | flops | bytes accessed | tf_op | source)
XLA Modules:
  0.0 258.1 jit_solution(1248480103618327704)
XLA Ops:
  15.8 3.8 %select_select_fusion = (bf16[16,64,8,64]{3,2,1,0:T(8,128)(2,1)}, bf16[16,64,8,64]{3,2,1,0:T(8,128)(2,1)}, bf16[16,64,8,64]{3,2,1,0:T(8,128)(2,1)S(1)}) fusion(bf16[16,64,8,64]{3,2,1,0:T(8,128)(2,1)} %squeeze.42, bf16[16,64,8,64]{3,2,1,0:T(8,128)(2,1)} %squeeze.40, pred[16,8]{1,0:T(8,128)(4,1)S(1)} %copy.20, pred[16,8]{1,0:T(8,128)(4,1)S(1)} %copy.19, ...), kind=kLoop, calls=%fused_computation.17 | loop fusion | flops 2621440 | bytes 5243264 | tf_op jit(solution)/shard_map/jit(_where)/select_n | solution.py:48
  21.6 11.9 %all_gather.3 = bf16[3,64,1024]{1,2,0:T(8,128)(2,1)S(1)} all-gather(bf16[3,64,128]{1,2,0:T(8,128)(2,1)S(1)} %pad_maximum_fusion), channel_id=1, replica_groups=mesh['obs'=4,'src'=8] {'src'}, dimensions={2}, use_global_device_ids=true | all-gather | bytes 442368 | tf_op jit(solution)/shard_map/all_gather | solution.py:61
  33.5 3.5 %select_n.221 = bf16[1024,512]{1,0:T(8,128)(2,1)S(1)} reshape(bf16[16,64,8,64]{3,2,1,0:T(8,128)(2,1)} %get-tuple-element.6) | data formatting | bytes 2097152 | tf_op jit(solution)/shard_map/jit(_where)/select_n | solution.py:48
  37.0 3.2 %select_n.224 = bf16[1024,512]{1,0:T(8,128)(2,1)S(1)} reshape(bf16[16,64,8,64]{3,2,1,0:T(8,128)(2,1)} %get-tuple-element.5) | data formatting | bytes 2097152 | tf_op jit(solution)/shard_map/jit(_where)/select_n | solution.py:48
  45.7 2.7 %broadcast_in_dim.38 = pred[1024,512]{1,0:T(32,128)(4,1)} reshape(pred[16,64,8,64]{3,2,1,0:T(8,128)(4,1)S(1)} %broadcast_in_dim.35) | data formatting | bytes 1048576 | tf_op jit(solution)/shard_map/jit(_where)/broadcast_in_dim | solution.py:48
  53.3 2.7 %bitcast_select_fusion = (bf16[1024,512]{1,0:T(8,128)(2,1)S(1)}, bf16[1024,512]{1,0:T(8,128)(2,1)S(1)}) fusion(pred[1024,512]{1,0:T(8,128)(4,1)} %broadcast_in_dim.39, pred[1024,512]{1,0:T(8,128)(4,1)} %broadcast_in_dim.40, bf16[128,8,4,128]{3,2,1,0:T(4,128)(2,1)} %bitcast.202, bf16[128,8,4,128]{3,2,1,0:T(4,128)(2,1)} %bitcast.197, ...), kind=kLoop, calls=%fused_computation.46 | loop fusion | flops 2097152 | bytes 5767168 | tf_op jit(solution)/shard_map/jit(_where)/select_n | solution.py:48
  57.9 5.2 %reduce-scatter.16.cloned.1.call-done = bf16[128,64]{1,0:T(8,128)(2,1)} async-done(((bf16[512,64]{1,0:T(8,128)(2,1)}), bf16[128,64]{1,0:T(8,128)(2,1)}) %reduce-scatter.16.cloned.1.call-update) | async-done | bytes 16400
  63.1 6.8 %bitcast_dynamic-update-slice_fusion.3 = (bf16[5,2,64,1536]{3,2,1,0:T(8,128)(2,1)}, bf16[2,64,1536]{2,1,0:T(8,128)(2,1)}) fusion(bf16[2,1536,1536]{2,1,0:T(8,128)(2,1)} %param.11, bf16[64,2,64]{0,2,1:T(8,128)(2,1)} %bitcast.208, bf16[2,64,1536]{2,1,0:T(8,128)(2,1)S(1)} %copy-done, bf16[5,2,64,1536]{3,2,1,0:T(8,128)(2,1)} %param.8), kind=kOutput, calls=%fused_computation.64 | convolution fusion | flops 629932032 | bytes 11042816 | tf_op jit(solution)/shard_map/ceb,cbd->ced/dot_general | solution.py:78
  72.7 2.6 %collective-permute-start.1 = (bf16[64,128]{1,0:T(8,128)(2,1)S(1)}, bf16[64,128]{1,0:T(8,128)(2,1)S(1)}, u32[]{:S(2)}, u32[]{:S(2)}) collective-permute-start(bf16[64,128]{1,0:T(8,128)(2,1)S(1)} %reshape.176), channel_id=1, source_target_pairs={{0,7},{1,0},{2,1},{3,2},{4,3},{5,4},{6,5},{7,6},{8,15},{9,8},{10,9... | collective-permute-start | bytes 49160 | tf_op jit(solution)/shard_map/ppermute | solution.py:25
  76.8 2.6 %collective-permute-start.3 = (bf16[64,128]{1,0:T(8,128)(2,1)S(1)}, bf16[64,128]{1,0:T(8,128)(2,1)S(1)}, u32[]{:S(2)}, u32[]{:S(2)}) collective-permute-start(bf16[64,128]{1,0:T(8,128)(2,1)S(1)} %collective-permute-done.1), channel_id=1, source_target_pairs={{0,7},{1,0},{2,1},{3,2},{4,3},{5,4},{6,5},{7,6},{8,15},{9,8},{10,9... | collective-permute-start | bytes 49160 | tf_op jit(solution)/shard_map/ppermute | solution.py:25
  80.9 2.6 %collective-permute-start.5 = (bf16[64,128]{1,0:T(8,128)(2,1)S(1)}, bf16[64,128]{1,0:T(8,128)(2,1)S(1)}, u32[]{:S(2)}, u32[]{:S(2)}) collective-permute-start(bf16[64,128]{1,0:T(8,128)(2,1)S(1)} %collective-permute-done.3), channel_id=1, source_target_pairs={{0,7},{1,0},{2,1},{3,2},{4,3},{5,4},{6,5},{7,6},{8,15},{9,8},{10,9... | collective-permute-start | bytes 49160 | tf_op jit(solution)/shard_map/ppermute | solution.py:25
  85.0 4.0 %collective-permute-done.6 = bf16[64,128]{1,0:T(8,128)(2,1)S(1)} collective-permute-done((bf16[64,128]{1,0:T(8,128)(2,1)S(1)}, bf16[64,128]{1,0:T(8,128)(2,1)S(1)}, u32[]{:S(2)}, u32[]{:S(2)}) %collective-permute-start.6) | collective-permute-done | bytes 16416 | tf_op jit(solution)/shard_map/ppermute | solution.py:20
  97.3 13.3 %reduce-scatter.18.cloned.1.call-done = bf16[128,64]{1,0:T(8,128)(2,1)} async-done(((bf16[512,64]{1,0:T(8,128)(2,1)}), bf16[128,64]{1,0:T(8,128)(2,1)}) %reduce-scatter.18.cloned.1.call-update) | async-done | bytes 16400
  110.6 6.7 %bitcast_dynamic-update-slice_fusion.2 = (bf16[5,2,64,1536]{3,2,1,0:T(8,128)(2,1)}, bf16[2,64,1536]{2,1,0:T(8,128)(2,1)}) fusion(bf16[5,2,64,1536]{3,2,1,0:T(8,128)(2,1)} %get-tuple-element.15, bf16[2,1536,1536]{2,1,0:T(8,128)(2,1)} %param.11, bf16[64,2,64]{0,2,1:T(8,128)(2,1)} %bitcast.209, bf16[2,64,1536]{2,1,0:T(8,128)(2,1)S(1)} %copy-done, ...), kind=kOutput, calls=%fused_computation.63 | convolution fusion | flops 629932032 | bytes 11042816 | tf_op jit(solution)/shard_map/ceb,cbd->ced/dot_general | solution.py:78
  120.2 2.6 %collective-permute-start.8 = (bf16[64,128]{1,0:T(8,128)(2,1)S(1)}, bf16[64,128]{1,0:T(8,128)(2,1)S(1)}, u32[]{:S(2)}, u32[]{:S(2)}) collective-permute-start(bf16[64,128]{1,0:T(8,128)(2,1)S(1)} %reshape.178), channel_id=1, source_target_pairs={{0,7},{1,0},{2,1},{3,2},{4,3},{5,4},{6,5},{7,6},{8,15},{9,8},{10,9... | collective-permute-start | bytes 49160 | tf_op jit(solution)/shard_map/ppermute | solution.py:25
  124.2 2.7 %collective-permute-start.10 = (bf16[64,128]{1,0:T(8,128)(2,1)S(1)}, bf16[64,128]{1,0:T(8,128)(2,1)S(1)}, u32[]{:S(2)}, u32[]{:S(2)}) collective-permute-start(bf16[64,128]{1,0:T(8,128)(2,1)S(1)} %collective-permute-done.8), channel_id=1, source_target_pairs={{0,7},{1,0},{2,1},{3,2},{4,3},{5,4},{6,5},{7,6},{8,15},{9,8},{10,9... | collective-permute-start | bytes 49160 | tf_op jit(solution)/shard_map/ppermute | solution.py:25
  128.4 2.6 %collective-permute-start.12 = (bf16[64,128]{1,0:T(8,128)(2,1)S(1)}, bf16[64,128]{1,0:T(8,128)(2,1)S(1)}, u32[]{:S(2)}, u32[]{:S(2)}) collective-permute-start(bf16[64,128]{1,0:T(8,128)(2,1)S(1)} %collective-permute-done.10), channel_id=1, source_target_pairs={{0,7},{1,0},{2,1},{3,2},{4,3},{5,4},{6,5},{7,6},{8,15},{9,8},{10,9... | collective-permute-start | bytes 49160 | tf_op jit(solution)/shard_map/ppermute | solution.py:25
  132.4 4.0 %collective-permute-done.13 = bf16[64,128]{1,0:T(8,128)(2,1)S(1)} collective-permute-done((bf16[64,128]{1,0:T(8,128)(2,1)S(1)}, bf16[64,128]{1,0:T(8,128)(2,1)S(1)}, u32[]{:S(2)}, u32[]{:S(2)}) %collective-permute-start.13) | collective-permute-done | bytes 16416 | tf_op jit(solution)/shard_map/ppermute | solution.py:20
  143.4 14.8 %reduce-scatter.20.cloned.1.call-done = bf16[128,64]{1,0:T(8,128)(2,1)} async-done(((bf16[512,64]{1,0:T(8,128)(2,1)}), bf16[128,64]{1,0:T(8,128)(2,1)}) %reduce-scatter.20.cloned.1.call-update) | async-done | bytes 16400
  158.2 6.7 %bitcast_dynamic-update-slice_fusion.1 = (bf16[5,2,64,1536]{3,2,1,0:T(8,128)(2,1)}, bf16[2,64,1536]{2,1,0:T(8,128)(2,1)}) fusion(bf16[5,2,64,1536]{3,2,1,0:T(8,128)(2,1)} %get-tuple-element.17, bf16[2,1536,1536]{2,1,0:T(8,128)(2,1)} %param.11, bf16[64,2,64]{0,2,1:T(8,128)(2,1)} %bitcast.210, bf16[2,64,1536]{2,1,0:T(8,128)(2,1)S(1)} %copy-done, ...), kind=kOutput, calls=%fused_computation.62 | convolution fusion | flops 629932032 | bytes 11042816 | tf_op jit(solution)/shard_map/ceb,cbd->ced/dot_general | solution.py:78
  166.4 2.6 %collective-permute-start.15 = (bf16[64,128]{1,0:T(8,128)(2,1)S(1)}, bf16[64,128]{1,0:T(8,128)(2,1)S(1)}, u32[]{:S(2)}, u32[]{:S(2)}) collective-permute-start(bf16[64,128]{1,0:T(8,128)(2,1)S(1)} %reshape.180), channel_id=1, source_target_pairs={{0,7},{1,0},{2,1},{3,2},{4,3},{5,4},{6,5},{7,6},{8,15},{9,8},{10,9... | collective-permute-start | bytes 49160 | tf_op jit(solution)/shard_map/ppermute | solution.py:25
  170.5 2.7 %collective-permute-start.17 = (bf16[64,128]{1,0:T(8,128)(2,1)S(1)}, bf16[64,128]{1,0:T(8,128)(2,1)S(1)}, u32[]{:S(2)}, u32[]{:S(2)}) collective-permute-start(bf16[64,128]{1,0:T(8,128)(2,1)S(1)} %collective-permute-done.15), channel_id=1, source_target_pairs={{0,7},{1,0},{2,1},{3,2},{4,3},{5,4},{6,5},{7,6},{8,15},{9,8},{10,9... | collective-permute-start | bytes 49160 | tf_op jit(solution)/shard_map/ppermute | solution.py:25
  174.6 2.6 %collective-permute-start.19 = (bf16[64,128]{1,0:T(8,128)(2,1)S(1)}, bf16[64,128]{1,0:T(8,128)(2,1)S(1)}, u32[]{:S(2)}, u32[]{:S(2)}) collective-permute-start(bf16[64,128]{1,0:T(8,128)(2,1)S(1)} %collective-permute-done.17), channel_id=1, source_target_pairs={{0,7},{1,0},{2,1},{3,2},{4,3},{5,4},{6,5},{7,6},{8,15},{9,8},{10,9... | collective-permute-start | bytes 49160 | tf_op jit(solution)/shard_map/ppermute | solution.py:25
  178.7 4.0 %collective-permute-done.20 = bf16[64,128]{1,0:T(8,128)(2,1)S(1)} collective-permute-done((bf16[64,128]{1,0:T(8,128)(2,1)S(1)}, bf16[64,128]{1,0:T(8,128)(2,1)S(1)}, u32[]{:S(2)}, u32[]{:S(2)}) %collective-permute-start.20) | collective-permute-done | bytes 16416 | tf_op jit(solution)/shard_map/ppermute | solution.py:20
  187.4 16.0 %reduce-scatter.22.cloned.1.call-done = bf16[128,64]{1,0:T(8,128)(2,1)} async-done(((bf16[512,64]{1,0:T(8,128)(2,1)}), bf16[128,64]{1,0:T(8,128)(2,1)}) %reduce-scatter.22.cloned.1.call-update) | async-done | bytes 16400
  203.4 6.6 %bitcast_dynamic-update-slice_fusion = (bf16[5,2,64,1536]{3,2,1,0:T(8,128)(2,1)}, bf16[2,64,1536]{2,1,0:T(8,128)(2,1)S(1)}) fusion(bf16[5,2,64,1536]{3,2,1,0:T(8,128)(2,1)} %get-tuple-element.19, bf16[2,1536,1536]{2,1,0:T(8,128)(2,1)} %param.11, bf16[64,2,64]{0,2,1:T(8,128)(2,1)} %bitcast.211, bf16[2,64,1536]{2,1,0:T(8,128)(2,1)S(1)} %copy-done, ...), kind=kOutput, calls=%fused_computation.61 | convolution fusion | flops 629932032 | bytes 11042816 | tf_op jit(solution)/shard_map/ceb,cbd->ced/dot_general | solution.py:78
  210.4 2.6 %collective-permute-start.22 = (bf16[64,128]{1,0:T(8,128)(2,1)S(1)}, bf16[64,128]{1,0:T(8,128)(2,1)S(1)}, u32[]{:S(2)}, u32[]{:S(2)}) collective-permute-start(bf16[64,128]{1,0:T(8,128)(2,1)S(1)} %reshape.182), channel_id=1, source_target_pairs={{0,7},{1,0},{2,1},{3,2},{4,3},{5,4},{6,5},{7,6},{8,15},{9,8},{10,9... | collective-permute-start | bytes 49160 | tf_op jit(solution)/shard_map/ppermute | solution.py:25
  214.5 2.7 %collective-permute-start.24 = (bf16[64,128]{1,0:T(8,128)(2,1)S(1)}, bf16[64,128]{1,0:T(8,128)(2,1)S(1)}, u32[]{:S(2)}, u32[]{:S(2)}) collective-permute-start(bf16[64,128]{1,0:T(8,128)(2,1)S(1)} %collective-permute-done.22), channel_id=1, source_target_pairs={{0,7},{1,0},{2,1},{3,2},{4,3},{5,4},{6,5},{7,6},{8,15},{9,8},{10,9... | collective-permute-start | bytes 49160 | tf_op jit(solution)/shard_map/ppermute | solution.py:25
  218.6 2.6 %collective-permute-start.26 = (bf16[64,128]{1,0:T(8,128)(2,1)S(1)}, bf16[64,128]{1,0:T(8,128)(2,1)S(1)}, u32[]{:S(2)}, u32[]{:S(2)}) collective-permute-start(bf16[64,128]{1,0:T(8,128)(2,1)S(1)} %collective-permute-done.24), channel_id=1, source_target_pairs={{0,7},{1,0},{2,1},{3,2},{4,3},{5,4},{6,5},{7,6},{8,15},{9,8},{10,9... | collective-permute-start | bytes 49160 | tf_op jit(solution)/shard_map/ppermute | solution.py:25
  222.7 4.0 %collective-permute-done.27 = bf16[64,128]{1,0:T(8,128)(2,1)S(1)} collective-permute-done((bf16[64,128]{1,0:T(8,128)(2,1)S(1)}, bf16[64,128]{1,0:T(8,128)(2,1)S(1)}, u32[]{:S(2)}, u32[]{:S(2)}) %collective-permute-start.27) | collective-permute-done | bytes 16416 | tf_op jit(solution)/shard_map/ppermute | solution.py:20
  228.0 17.1 %reduce-scatter.24.cloned.1.call-done = bf16[128,64]{1,0:T(8,128)(2,1)} async-done(((bf16[512,64]{1,0:T(8,128)(2,1)}), bf16[128,64]{1,0:T(8,128)(2,1)}) %reduce-scatter.24.cloned.1.call-update) | async-done | bytes 16400
  245.1 6.5 %fusion.6 = bf16[5,2,64,1536]{3,2,1,0:T(8,128)(2,1)} fusion(bf16[5,2,64,1536]{3,2,1,0:T(8,128)(2,1)} %get-tuple-element.21, bf16[2,1536,1536]{2,1,0:T(8,128)(2,1)} %param.11, bf16[64,2,64]{0,2,1:T(8,128)(2,1)} %bitcast.212, bf16[2,64,1536]{2,1,0:T(8,128)(2,1)S(1)} %copy-done, bf16[5,2,64,1536]{3,2,1,0:T(8,128)(2,1)} %param.8), kind=kOutput, calls=%fused_computation.16 | convolution fusion | flops 629932032 | bytes 10649600 | tf_op jit(solution)/shard_map/ceb,cbd->ced/dot_general | solution.py:78
  (164 shorter events, 69.7 us)
Async XLA Ops:
  6.5 56.5 %reduce-scatter.16.cloned.1.call-start = ((), (), s32[]{:S(2)}) async-start(), calls=%async_computation.5 | async-start | bytes 163840
  43.2 67.4 %reduce-scatter.18.cloned.1.call-start = ((), (), s32[]{:S(2)}) async-start(), calls=%async_computation.6 | async-start | bytes 163840
  72.7 4.1 %collective-permute-start = (bf16[64,128]{1,0:T(8,128)(2,1)S(1)}, bf16[64,128]{1,0:T(8,128)(2,1)S(1)}, u32[]{:S(2)}, u32[]{:S(2)}) collective-permute-start(bf16[64,128]{1,0:T(8,128)(2,1)S(1)} %reshape.176), channel_id=1, source_target_pairs={{0,1},{1,2},{2,3},{3,4},{4,5},{5,6},{6,7},{7,0},{8,9},{9,10},{10,1... | collective-permute-start | bytes 49160 | tf_op jit(solution)/shard_map/ppermute | solution.py:20
  72.7 4.1 %collective-permute-start.1 = (bf16[64,128]{1,0:T(8,128)(2,1)S(1)}, bf16[64,128]{1,0:T(8,128)(2,1)S(1)}, u32[]{:S(2)}, u32[]{:S(2)}) collective-permute-start(bf16[64,128]{1,0:T(8,128)(2,1)S(1)} %reshape.176), channel_id=1, source_target_pairs={{0,7},{1,0},{2,1},{3,2},{4,3},{5,4},{6,5},{7,6},{8,15},{9,8},{10,9... | collective-permute-start | bytes 49160 | tf_op jit(solution)/shard_map/ppermute | solution.py:25
  76.8 4.1 %collective-permute-start.2 = (bf16[64,128]{1,0:T(8,128)(2,1)S(1)}, bf16[64,128]{1,0:T(8,128)(2,1)S(1)}, u32[]{:S(2)}, u32[]{:S(2)}) collective-permute-start(bf16[64,128]{1,0:T(8,128)(2,1)S(1)} %collective-permute-done), channel_id=1, source_target_pairs={{0,1},{1,2},{2,3},{3,4},{4,5},{5,6},{6,7},{7,0},{8,9},{9,10},{10,1... | collective-permute-start | bytes 49160 | tf_op jit(solution)/shard_map/ppermute | solution.py:20
  76.8 4.1 %collective-permute-start.3 = (bf16[64,128]{1,0:T(8,128)(2,1)S(1)}, bf16[64,128]{1,0:T(8,128)(2,1)S(1)}, u32[]{:S(2)}, u32[]{:S(2)}) collective-permute-start(bf16[64,128]{1,0:T(8,128)(2,1)S(1)} %collective-permute-done.1), channel_id=1, source_target_pairs={{0,7},{1,0},{2,1},{3,2},{4,3},{5,4},{6,5},{7,6},{8,15},{9,8},{10,9... | collective-permute-start | bytes 49160 | tf_op jit(solution)/shard_map/ppermute | solution.py:25
  80.9 4.1 %collective-permute-start.4 = (bf16[64,128]{1,0:T(8,128)(2,1)S(1)}, bf16[64,128]{1,0:T(8,128)(2,1)S(1)}, u32[]{:S(2)}, u32[]{:S(2)}) collective-permute-start(bf16[64,128]{1,0:T(8,128)(2,1)S(1)} %collective-permute-done.2), channel_id=1, source_target_pairs={{0,1},{1,2},{2,3},{3,4},{4,5},{5,6},{6,7},{7,0},{8,9},{9,10},{10,1... | collective-permute-start | bytes 49160 | tf_op jit(solution)/shard_map/ppermute | solution.py:20
  80.9 4.1 %collective-permute-start.5 = (bf16[64,128]{1,0:T(8,128)(2,1)S(1)}, bf16[64,128]{1,0:T(8,128)(2,1)S(1)}, u32[]{:S(2)}, u32[]{:S(2)}) collective-permute-start(bf16[64,128]{1,0:T(8,128)(2,1)S(1)} %collective-permute-done.3), channel_id=1, source_target_pairs={{0,7},{1,0},{2,1},{3,2},{4,3},{5,4},{6,5},{7,6},{8,15},{9,8},{10,9... | collective-permute-start | bytes 49160 | tf_op jit(solution)/shard_map/ppermute | solution.py:25
  84.9 4.1 %collective-permute-start.6 = (bf16[64,128]{1,0:T(8,128)(2,1)S(1)}, bf16[64,128]{1,0:T(8,128)(2,1)S(1)}, u32[]{:S(2)}, u32[]{:S(2)}) collective-permute-start(bf16[64,128]{1,0:T(8,128)(2,1)S(1)} %collective-permute-done.4), channel_id=1, source_target_pairs={{0,1},{1,2},{2,3},{3,4},{4,5},{5,6},{6,7},{7,0},{8,9},{9,10},{10,1... | collective-permute-start | bytes 49160 | tf_op jit(solution)/shard_map/ppermute | solution.py:20
  93.5 64.7 %reduce-scatter.20.cloned.1.call-start = ((), (), s32[]{:S(2)}) async-start(), calls=%async_computation.7 | async-start | bytes 163840
  120.1 4.1 %collective-permute-start.7 = (bf16[64,128]{1,0:T(8,128)(2,1)S(1)}, bf16[64,128]{1,0:T(8,128)(2,1)S(1)}, u32[]{:S(2)}, u32[]{:S(2)}) collective-permute-start(bf16[64,128]{1,0:T(8,128)(2,1)S(1)} %reshape.178), channel_id=1, source_target_pairs={{0,1},{1,2},{2,3},{3,4},{4,5},{5,6},{6,7},{7,0},{8,9},{9,10},{10,1... | collective-permute-start | bytes 49160 | tf_op jit(solution)/shard_map/ppermute | solution.py:20
  120.2 4.1 %collective-permute-start.8 = (bf16[64,128]{1,0:T(8,128)(2,1)S(1)}, bf16[64,128]{1,0:T(8,128)(2,1)S(1)}, u32[]{:S(2)}, u32[]{:S(2)}) collective-permute-start(bf16[64,128]{1,0:T(8,128)(2,1)S(1)} %reshape.178), channel_id=1, source_target_pairs={{0,7},{1,0},{2,1},{3,2},{4,3},{5,4},{6,5},{7,6},{8,15},{9,8},{10,9... | collective-permute-start | bytes 49160 | tf_op jit(solution)/shard_map/ppermute | solution.py:25
  124.2 4.1 %collective-permute-start.9 = (bf16[64,128]{1,0:T(8,128)(2,1)S(1)}, bf16[64,128]{1,0:T(8,128)(2,1)S(1)}, u32[]{:S(2)}, u32[]{:S(2)}) collective-permute-start(bf16[64,128]{1,0:T(8,128)(2,1)S(1)} %collective-permute-done.7), channel_id=1, source_target_pairs={{0,1},{1,2},{2,3},{3,4},{4,5},{5,6},{6,7},{7,0},{8,9},{9,10},{10,1... | collective-permute-start | bytes 49160 | tf_op jit(solution)/shard_map/ppermute | solution.py:20
  124.2 4.1 %collective-permute-start.10 = (bf16[64,128]{1,0:T(8,128)(2,1)S(1)}, bf16[64,128]{1,0:T(8,128)(2,1)S(1)}, u32[]{:S(2)}, u32[]{:S(2)}) collective-permute-start(bf16[64,128]{1,0:T(8,128)(2,1)S(1)} %collective-permute-done.8), channel_id=1, source_target_pairs={{0,7},{1,0},{2,1},{3,2},{4,3},{5,4},{6,5},{7,6},{8,15},{9,8},{10,9... | collective-permute-start | bytes 49160 | tf_op jit(solution)/shard_map/ppermute | solution.py:25
  128.3 4.1 %collective-permute-start.11 = (bf16[64,128]{1,0:T(8,128)(2,1)S(1)}, bf16[64,128]{1,0:T(8,128)(2,1)S(1)}, u32[]{:S(2)}, u32[]{:S(2)}) collective-permute-start(bf16[64,128]{1,0:T(8,128)(2,1)S(1)} %collective-permute-done.9), channel_id=1, source_target_pairs={{0,1},{1,2},{2,3},{3,4},{4,5},{5,6},{6,7},{7,0},{8,9},{9,10},{10,1... | collective-permute-start | bytes 49160 | tf_op jit(solution)/shard_map/ppermute | solution.py:20
  128.4 4.1 %collective-permute-start.12 = (bf16[64,128]{1,0:T(8,128)(2,1)S(1)}, bf16[64,128]{1,0:T(8,128)(2,1)S(1)}, u32[]{:S(2)}, u32[]{:S(2)}) collective-permute-start(bf16[64,128]{1,0:T(8,128)(2,1)S(1)} %collective-permute-done.10), channel_id=1, source_target_pairs={{0,7},{1,0},{2,1},{3,2},{4,3},{5,4},{6,5},{7,6},{8,15},{9,8},{10,9... | collective-permute-start | bytes 49160 | tf_op jit(solution)/shard_map/ppermute | solution.py:25
  132.3 4.1 %collective-permute-start.13 = (bf16[64,128]{1,0:T(8,128)(2,1)S(1)}, bf16[64,128]{1,0:T(8,128)(2,1)S(1)}, u32[]{:S(2)}, u32[]{:S(2)}) collective-permute-start(bf16[64,128]{1,0:T(8,128)(2,1)S(1)} %collective-permute-done.11), channel_id=1, source_target_pairs={{0,1},{1,2},{2,3},{3,4},{4,5},{5,6},{6,7},{7,0},{8,9},{9,10},{10,1... | collective-permute-start | bytes 49160 | tf_op jit(solution)/shard_map/ppermute | solution.py:20
  141.2 62.1 %reduce-scatter.22.cloned.1.call-start = ((), (), s32[]{:S(2)}) async-start(), calls=%async_computation.8 | async-start | bytes 163840
  166.3 4.1 %collective-permute-start.14 = (bf16[64,128]{1,0:T(8,128)(2,1)S(1)}, bf16[64,128]{1,0:T(8,128)(2,1)S(1)}, u32[]{:S(2)}, u32[]{:S(2)}) collective-permute-start(bf16[64,128]{1,0:T(8,128)(2,1)S(1)} %reshape.180), channel_id=1, source_target_pairs={{0,1},{1,2},{2,3},{3,4},{4,5},{5,6},{6,7},{7,0},{8,9},{9,10},{10,1... | collective-permute-start | bytes 49160 | tf_op jit(solution)/shard_map/ppermute | solution.py:20
  166.4 4.1 %collective-permute-start.15 = (bf16[64,128]{1,0:T(8,128)(2,1)S(1)}, bf16[64,128]{1,0:T(8,128)(2,1)S(1)}, u32[]{:S(2)}, u32[]{:S(2)}) collective-permute-start(bf16[64,128]{1,0:T(8,128)(2,1)S(1)} %reshape.180), channel_id=1, source_target_pairs={{0,7},{1,0},{2,1},{3,2},{4,3},{5,4},{6,5},{7,6},{8,15},{9,8},{10,9... | collective-permute-start | bytes 49160 | tf_op jit(solution)/shard_map/ppermute | solution.py:25
  170.4 4.1 %collective-permute-start.16 = (bf16[64,128]{1,0:T(8,128)(2,1)S(1)}, bf16[64,128]{1,0:T(8,128)(2,1)S(1)}, u32[]{:S(2)}, u32[]{:S(2)}) collective-permute-start(bf16[64,128]{1,0:T(8,128)(2,1)S(1)} %collective-permute-done.14), channel_id=1, source_target_pairs={{0,1},{1,2},{2,3},{3,4},{4,5},{5,6},{6,7},{7,0},{8,9},{9,10},{10,1... | collective-permute-start | bytes 49160 | tf_op jit(solution)/shard_map/ppermute | solution.py:20
  170.5 4.1 %collective-permute-start.17 = (bf16[64,128]{1,0:T(8,128)(2,1)S(1)}, bf16[64,128]{1,0:T(8,128)(2,1)S(1)}, u32[]{:S(2)}, u32[]{:S(2)}) collective-permute-start(bf16[64,128]{1,0:T(8,128)(2,1)S(1)} %collective-permute-done.15), channel_id=1, source_target_pairs={{0,7},{1,0},{2,1},{3,2},{4,3},{5,4},{6,5},{7,6},{8,15},{9,8},{10,9... | collective-permute-start | bytes 49160 | tf_op jit(solution)/shard_map/ppermute | solution.py:25
  174.5 4.1 %collective-permute-start.18 = (bf16[64,128]{1,0:T(8,128)(2,1)S(1)}, bf16[64,128]{1,0:T(8,128)(2,1)S(1)}, u32[]{:S(2)}, u32[]{:S(2)}) collective-permute-start(bf16[64,128]{1,0:T(8,128)(2,1)S(1)} %collective-permute-done.16), channel_id=1, source_target_pairs={{0,1},{1,2},{2,3},{3,4},{4,5},{5,6},{6,7},{7,0},{8,9},{9,10},{10,1... | collective-permute-start | bytes 49160 | tf_op jit(solution)/shard_map/ppermute | solution.py:20
  178.6 4.1 %collective-permute-start.20 = (bf16[64,128]{1,0:T(8,128)(2,1)S(1)}, bf16[64,128]{1,0:T(8,128)(2,1)S(1)}, u32[]{:S(2)}, u32[]{:S(2)}) collective-permute-start(bf16[64,128]{1,0:T(8,128)(2,1)S(1)} %collective-permute-done.18), channel_id=1, source_target_pairs={{0,1},{1,2},{2,3},{3,4},{4,5},{5,6},{6,7},{7,0},{8,9},{9,10},{10,1... | collective-permute-start | bytes 49160 | tf_op jit(solution)/shard_map/ppermute | solution.py:20
  186.4 58.7 %reduce-scatter.24.cloned.1.call-start = ((), (), s32[]{:S(2)}) async-start(), calls=%async_computation.9 | async-start | bytes 163840
  210.3 4.1 %collective-permute-start.21 = (bf16[64,128]{1,0:T(8,128)(2,1)S(1)}, bf16[64,128]{1,0:T(8,128)(2,1)S(1)}, u32[]{:S(2)}, u32[]{:S(2)}) collective-permute-start(bf16[64,128]{1,0:T(8,128)(2,1)S(1)} %reshape.182), channel_id=1, source_target_pairs={{0,1},{1,2},{2,3},{3,4},{4,5},{5,6},{6,7},{7,0},{8,9},{9,10},{10,1... | collective-permute-start | bytes 49160 | tf_op jit(solution)/shard_map/ppermute | solution.py:20
  210.4 4.1 %collective-permute-start.22 = (bf16[64,128]{1,0:T(8,128)(2,1)S(1)}, bf16[64,128]{1,0:T(8,128)(2,1)S(1)}, u32[]{:S(2)}, u32[]{:S(2)}) collective-permute-start(bf16[64,128]{1,0:T(8,128)(2,1)S(1)} %reshape.182), channel_id=1, source_target_pairs={{0,7},{1,0},{2,1},{3,2},{4,3},{5,4},{6,5},{7,6},{8,15},{9,8},{10,9... | collective-permute-start | bytes 49160 | tf_op jit(solution)/shard_map/ppermute | solution.py:25
  214.5 4.1 %collective-permute-start.23 = (bf16[64,128]{1,0:T(8,128)(2,1)S(1)}, bf16[64,128]{1,0:T(8,128)(2,1)S(1)}, u32[]{:S(2)}, u32[]{:S(2)}) collective-permute-start(bf16[64,128]{1,0:T(8,128)(2,1)S(1)} %collective-permute-done.21), channel_id=1, source_target_pairs={{0,1},{1,2},{2,3},{3,4},{4,5},{5,6},{6,7},{7,0},{8,9},{9,10},{10,1... | collective-permute-start | bytes 49160 | tf_op jit(solution)/shard_map/ppermute | solution.py:20
  214.5 4.1 %collective-permute-start.24 = (bf16[64,128]{1,0:T(8,128)(2,1)S(1)}, bf16[64,128]{1,0:T(8,128)(2,1)S(1)}, u32[]{:S(2)}, u32[]{:S(2)}) collective-permute-start(bf16[64,128]{1,0:T(8,128)(2,1)S(1)} %collective-permute-done.22), channel_id=1, source_target_pairs={{0,7},{1,0},{2,1},{3,2},{4,3},{5,4},{6,5},{7,6},{8,15},{9,8},{10,9... | collective-permute-start | bytes 49160 | tf_op jit(solution)/shard_map/ppermute | solution.py:25
  218.5 4.1 %collective-permute-start.25 = (bf16[64,128]{1,0:T(8,128)(2,1)S(1)}, bf16[64,128]{1,0:T(8,128)(2,1)S(1)}, u32[]{:S(2)}, u32[]{:S(2)}) collective-permute-start(bf16[64,128]{1,0:T(8,128)(2,1)S(1)} %collective-permute-done.23), channel_id=1, source_target_pairs={{0,1},{1,2},{2,3},{3,4},{4,5},{5,6},{6,7},{7,0},{8,9},{9,10},{10,1... | collective-permute-start | bytes 49160 | tf_op jit(solution)/shard_map/ppermute | solution.py:20
  218.6 4.1 %collective-permute-start.26 = (bf16[64,128]{1,0:T(8,128)(2,1)S(1)}, bf16[64,128]{1,0:T(8,128)(2,1)S(1)}, u32[]{:S(2)}, u32[]{:S(2)}) collective-permute-start(bf16[64,128]{1,0:T(8,128)(2,1)S(1)} %collective-permute-done.24), channel_id=1, source_target_pairs={{0,7},{1,0},{2,1},{3,2},{4,3},{5,4},{6,5},{7,6},{8,15},{9,8},{10,9... | collective-permute-start | bytes 49160 | tf_op jit(solution)/shard_map/ppermute | solution.py:25
  222.6 4.1 %collective-permute-start.27 = (bf16[64,128]{1,0:T(8,128)(2,1)S(1)}, bf16[64,128]{1,0:T(8,128)(2,1)S(1)}, u32[]{:S(2)}, u32[]{:S(2)}) collective-permute-start(bf16[64,128]{1,0:T(8,128)(2,1)S(1)} %collective-permute-done.25), channel_id=1, source_target_pairs={{0,1},{1,2},{2,3},{3,4},{4,5},{5,6},{6,7},{7,0},{8,9},{9,10},{10,1... | collective-permute-start | bytes 49160 | tf_op jit(solution)/shard_map/ppermute | solution.py:20
  (14 other events, 191.3 us)
Sparse Core Ops, SparseCore 0:
  43.3 19.7 reduce-scatter.15
  93.7 16.8 reduce-scatter.17
  141.4 16.7 reduce-scatter.19
  186.5 16.8 reduce-scatter.21
  228.1 16.9 reduce-scatter.23
